TPU v7x, 256 devices: a whole 4x4x8 slice. The times are simulated.
256 devices in a mesh: wall: 16 (over y, x_lo, core), span: 16 (over x_hi, z).
Axes of the slice: x: 4 (x_hi: 2, x_lo: 2; x = x_hi * 2 + x_lo), y: 4, z: 8, core: 2. Of those that a mesh axis runs over, the one named last changes fastest.
Arguments:
- field: float32 [4, 3, 2, 512, 6144], P(None, None, None, 'wall', 'span'), may hold values from -6 to 6
- mean_flow: float32 [2, 512], P(None, 'wall'), may hold values from 0.2 to 1.5
- d2_coef: float32 [15, 512], P(None, 'wall'), may hold values from -2 to 2
- wall_coef: float32 [2, 8], replicated, may hold values from -0.4375 to 0.4375
- kx_index: int32 [4], replicated, may hold values from 1 to 7
- patch_of: int32 [6144], P('span'), may hold values from 0 to 63
Outputs:
- new_field: float32 [4, 3, 2, 512, 6144], P(None, None, None, 'wall', 'span')
- wall_grad: float32 [2, 4, 2, 64], replicated
All inputs are finite; a program needn't handle non-finite values.
Results may differ from a plain program's by a relative error of at most 0.000073.
Values sent between devices are 32-bit elements; how exact they have to be, the bound alone decides.
A program may use at most 128 MiB of HBM per device.

v0:
```python
import math

import jax
import jax.numpy as jnp
from jax import lax
from jax.sharding import PartitionSpec as P

HALO = 7
STEN = 15
PATCH = 64


TAU = 0.25
VIS = 0.5


def with_halo(block, sides, width):
    for axis, dim in sides:
        count = lax.axis_size(axis)
        forward = [(i, i + 1) for i in range(count - 1)]
        backward = [(target, source) for source, target in forward]
        low = lax.ppermute(
            lax.slice_in_dim(block, block.shape[dim] - width, None, axis=dim), axis, forward
        )
        high = lax.ppermute(lax.slice_in_dim(block, 0, width, axis=dim), axis, backward)
        block = jnp.concatenate([low, block, high], axis=dim)
    return block


def spanwise_operator(line_data):
    item_count, part_count, row_count, length = line_data.shape
    inner_size = 128
    outer_size = length // inner_size
    highest = lax.Precision.HIGHEST
    real_part = line_data[:, 0].reshape(item_count, row_count, outer_size, inner_size)
    imag_part = line_data[:, 1].reshape(item_count, row_count, outer_size, inner_size)
    outer = jnp.arange(outer_size, dtype=jnp.int32)
    inner = jnp.arange(inner_size, dtype=jnp.int32)
    angle_one = (
        -2.0
        * math.pi
        / outer_size
        * (outer[:, None] * outer[None, :] % outer_size).astype(jnp.float32)
    )
    angle_two = (
        -2.0
        * math.pi
        / inner_size
        * (inner[:, None] * inner[None, :] % inner_size).astype(jnp.float32)
    )
    angle_twist = (
        -2.0 * math.pi / length * (outer[:, None] * inner[None, :] % length).astype(jnp.float32)
    )
    cos_one, sin_one = (jnp.cos(angle_one), jnp.sin(angle_one))
    cos_two, sin_two = (jnp.cos(angle_two), jnp.sin(angle_two))
    cos_twist, sin_twist = (jnp.cos(angle_twist), jnp.sin(angle_twist))

    def first_section(table, values):
        return jnp.einsum("kn,irnm->irkm", table, values, precision=highest)

    def second_section(values, table):
        return jnp.einsum("irkn,nm->irkm", values, table, precision=highest)

    def second_back(values, table):
        return jnp.einsum("irkm,nm->irkn", values, table, precision=highest)

    def first_back(table, values):
        return jnp.einsum("kn,irkm->irnm", table, values, precision=highest)

    section_real = first_section(cos_one, real_part) - first_section(sin_one, imag_part)
    section_imag = first_section(cos_one, imag_part) + first_section(sin_one, real_part)
    twist_real = section_real * cos_twist - section_imag * sin_twist
    twist_imag = section_real * sin_twist + section_imag * cos_twist
    modes_real = second_section(twist_real, cos_two) - second_section(twist_imag, sin_two)
    modes_imag = second_section(twist_real, sin_two) + second_section(twist_imag, cos_two)
    wave_index = outer[:, None] + outer_size * inner[None, :]
    signed = jnp.where(wave_index > length // 2, wave_index - length, wave_index)
    cutoff = length // 3
    wave_ratio = signed.astype(jnp.float32) / cutoff
    multiplier = jnp.where(
        jnp.abs(signed) < cutoff, -VIS * wave_ratio * wave_ratio, 0.0 * wave_ratio
    )
    modes_real = modes_real * multiplier
    modes_imag = modes_imag * multiplier
    back_real = second_back(modes_real, cos_two) + second_back(modes_imag, sin_two)
    back_imag = second_back(modes_imag, cos_two) - second_back(modes_real, sin_two)
    untwist_real = back_real * cos_twist + back_imag * sin_twist
    untwist_imag = back_imag * cos_twist - back_real * sin_twist
    result_real = (first_back(cos_one, untwist_real) + first_back(sin_one, untwist_imag)) / length
    result_imag = (first_back(cos_one, untwist_imag) - first_back(sin_one, untwist_real)) / length
    result_real = result_real.reshape(item_count, row_count, length)
    result_imag = result_imag.reshape(item_count, row_count, length)
    return jnp.stack([result_real, result_imag], axis=1)


def on_device(field, mean_flow, d2_coef, wall_coef, kx_index, patch_of):
    mode_count, comp_count, part_count, row_count, col_count = field.shape
    padded = with_halo(field, (("wall", 3),), HALO)
    diffusion = jnp.zeros_like(field)
    for offset in range(STEN):
        diffusion = (
            diffusion + d2_coef[offset][:, None] * padded[:, :, :, offset : offset + row_count, :]
        )
    flattened = field.reshape(mode_count * comp_count, part_count, row_count, col_count)
    spectral_lines = spanwise_operator(
        lax.all_to_all(flattened, "span", split_axis=2, concat_axis=3, tiled=True)
    )
    spanwise = lax.all_to_all(spectral_lines, "span", split_axis=3, concat_axis=2, tiled=True)
    spanwise = spanwise.reshape(field.shape)
    wave_number = kx_index.astype(jnp.float32) * 0.25
    velocity = mean_flow[0]
    shear_rate = mean_flow[1]
    advect_rate = wave_number[:, None, None, None] * velocity[None, None, :, None]
    advect_real = -advect_rate * field[:, :, 1]
    advect_imag = advect_rate * field[:, :, 0]
    advection = jnp.stack([advect_real, advect_imag], axis=2)
    coupling = shear_rate[None, None, :, None] * field[:, 0]
    advection = advection.at[:, 1].add(-coupling)
    new_field = field + TAU * advection + diffusion + spanwise
    lower_wall = jnp.zeros_like(new_field[:, 0, :, 0, :])
    upper_wall = jnp.zeros_like(new_field[:, 0, :, 0, :])
    for offset in range(HALO + 1):
        lower_wall = lower_wall + wall_coef[0, offset] * new_field[:, 0, :, offset, :]
        upper_wall = (
            upper_wall + wall_coef[1, offset] * new_field[:, 0, :, row_count - 1 - offset, :]
        )
    wall_index = lax.axis_index("wall")
    wall_count = lax.axis_size("wall")
    lower_wall = jnp.where(wall_index == 0, lower_wall, 0.0 * lower_wall)
    upper_wall = jnp.where(wall_index == wall_count - 1, upper_wall, 0.0 * upper_wall)
    shear_rows = jnp.stack([lower_wall, upper_wall])
    onehot = (patch_of[:, None] == jnp.arange(PATCH, dtype=jnp.int32)[None, :]).astype(jnp.float32)
    partial_grad = jnp.einsum("wmcz,zp->wmcp", shear_rows, onehot, precision=lax.Precision.HIGHEST)
    wall_grad = lax.psum(partial_grad, ("wall", "span"))
    return (new_field, wall_grad)


def solution(mesh):
    return jax.shard_map(
        on_device,
        mesh=mesh,
        in_specs=(
            P(None, None, None, "wall", "span"),
            P(None, "wall"),
            P(None, "wall"),
            P(),
            P(),
            P("span"),
        ),
        out_specs=(P(None, None, None, "wall", "span"), P()),
        check_vma=False,
    )
```

profile of v0, /device:TPU:1, one launch (start us, length us, event | category | flops | bytes accessed | tf_op | source)
XLA Modules:
  0.0 284.4 jit_solution(1954556570748203936)
XLA Ops:
  0.6 3.2 %copy.115 = f32[4,3,2,32,384]{4,2,1,0,3:T(2,128)} copy(f32[4,3,2,32,384]{4,3,2,1,0:T(8,128)} %param.8) | data formatting | bytes 2359296 | tf_op args[0]
  3.8 11.7 %all-to-all-start = ((f32[12,2,32,384]{3,1,0,2:T(2,128)}), f32[12,2,32,384]{3,1,0,2:T(2,128)S(1)}, u32[]{:S(2)}, u32[]{:S(2)}) async-start(f32[12,2,32,384]{3,1,0,2:T(2,128)} %bitcast.18), calls=%async_computation | async-start | bytes 2359296 | tf_op jit(solution)/shard_map/all_to_all | solution.py:106
  17.2 3.0 %collective-permute-start = (f32[4,3,2,7,384]{4,0,2,3,1:T(4,128)}, f32[4,3,2,7,384]{4,0,2,3,1:T(4,128)}, u32[]{:S(2)}, u32[]{:S(2)}) collective-permute-start(f32[4,3,2,7,384]{4,0,2,3,1:T(4,128)} %get-tuple-element.32), channel_id=1, source_target_pairs={{0,16},{16,32},{32,48},{48,64},{64,80},{80,96},{96,112},{112,128},... | collective-permute-start | bytes 774152 | tf_op jit(solution)/shard_map/ppermute | solution.py:22
  20.3 2.0 collective-permute-start.1
  23.6 21.4 %all-to-all-done = f32[12,2,32,384]{3,1,0,2:T(2,128)S(1)} async-done(((f32[12,2,32,384]{3,1,0,2:T(2,128)}), f32[12,2,32,384]{3,1,0,2:T(2,128)S(1)}, u32[]{:S(2)}, u32[]{:S(2)}) %all-to-all-start) | async-done | bytes 1179680 | tf_op jit(solution)/shard_map/all_to_all | solution.py:106
  45.0 1.4 copy.116
  46.4 2.1 all_to_all.27
  60.6 1.0 fusion.33
  62.5 4.5 %copy.141 = f32[12,2,48,128]{0,1,3,2:T(2,128)} copy(f32[12,2,48,128]{3,2,1,0:T(8,128)S(1)} %fusion.3) | data formatting | bytes 1179648 | tf_op jit(solution)/shard_map/stack;reshape | solution.py:93
  67.0 1.6 fusion.1
  68.6 4.6 %copy.142 = f32[12,2,48,128]{0,1,3,2:T(2,128)} copy(f32[12,2,48,128]{3,2,1,0:T(8,128)S(1)} %fusion.1) | data formatting | bytes 1179648 | tf_op jit(solution)/shard_map/stack;reshape | solution.py:93
  73.2 11.8 %fusion.200 = f32[6144,2,2,12]{3,2,1,0:T(2,128)} fusion(f32[12,1,2,6144]{0,2,1,3:T(2,128)} %bitcast.155, f32[12,1,2,6144]{0,2,1,3:T(2,128)} %bitcast.154), kind=kLoop, calls=%fused_computation.261 | loop fusion | flops 294912 | bytes 2359296
  85.0 22.7 %reshape.465 = f32[16,1,18432]{2,1,0:T(1,128)} reshape(f32[6144,2,2,12]{3,2,1,0:T(2,128)} %fusion.200) | data formatting | bytes 2359296
  107.7 6.6 %all-to-all-start.1 = ((f32[16,1,18432]{2,1,0:T(1,128)}), f32[16,1,18432]{2,1,0:T(1,128)}, u32[]{:S(2)}, u32[]{:S(2)}) async-start(f32[16,1,18432]{2,1,0:T(1,128)} %reshape.465), calls=%async_computation.1 | async-start | bytes 2359296 | tf_op jit(solution)/shard_map/all_to_all | solution.py:108
  122.3 21.7 %all-to-all-done.1 = f32[16,1,18432]{2,1,0:T(1,128)} async-done(((f32[16,1,18432]{2,1,0:T(1,128)}), f32[16,1,18432]{2,1,0:T(1,128)}, u32[]{:S(2)}, u32[]{:S(2)}) %all-to-all-start.1) | async-done | bytes 1179680 | tf_op jit(solution)/shard_map/all_to_all | solution.py:108
  144.5 5.7 %reduce.2 = f32[16,18432]{1,0:T(8,128)} reduce(f32[16,1,18432]{2,1,0:T(1,128)} %all-to-all-done.1, f32[]{:T(128)} %broadcast.394), dimensions={1}, to_apply=%all_to_all.28.reduce_sub_computation | reduce | bytes 2359300 | tf_op jit(solution)/shard_map/all_to_all | solution.py:108
  150.2 27.5 %reshape.466 = f32[6144,2,2,12]{3,2,1,0:T(2,128)} reshape(f32[16,18432]{1,0:T(8,128)} %reduce.2) | data formatting | bytes 2359296
  177.7 11.2 %copy.143 = f32[12,2,2,16,384]{4,3,2,1,0:T(8,128)} copy(f32[12,2,2,16,384]{0,2,1,4,3:T(2,128)} %bitcast.153) | data formatting | bytes 2359296 | tf_op jit(solution)/shard_map/all_to_all | solution.py:108
  188.9 2.3 copy.124
  191.4 4.5 %fusion.8 = f32[4,3,2,32,384]{4,0,2,3,1:T(4,128)S(1)} fusion(f32[4,3,2,39,384]{4,0,2,3,1:T(4,128)S(1)} %constant_dynamic-update-slice_fusion.2, f32[4,3,2,39,384]{4,0,2,3,1:T(4,128)S(1)} %get-tuple-element.30, f32[4,3,2,32,384]{4,2,3,1,0:T(2,128)S(1)} %bitcast.156, f32[4,3,2,32,384]{4,0,2,3,1:T(4,128)S(1)} %copy-done.4, f32[32]{0:T(128)S(1)} %copy-done.19, ...), kind=kLoop, calls=%fused_computation.21 | loop fusion | flops 9732096 | bytes 21235584 | tf_op jit(solution)/shard_map/add | solution.py:119
  195.9 1.2 copy.126
  197.1 5.2 %multiply_select_fusion.1 = f32[1,4,2,384]{3,1,2,0:T(4,128)S(1)} fusion(f32[4,3,2,32,384]{4,0,2,3,1:T(4,128)S(1)} %fusion.8, f32[]{:T(128)} %bitcast.61, f32[]{:T(128)} %bitcast.60, f32[]{:T(128)} %bitcast.59, f32[]{:T(128)} %bitcast.58, f32[]{:T(128)} %bitcast.57, f32[]{:T(128)} %bitcast.56, f32[]{:T(128)} %bitcast.55, f32[]{:T(128)} %bitcast.54, pred[]{:T(512)S(6)} %eq.26), kind=kLoop, calls=%fused_computation.126 | loop fusion | flops 52224 | bytes 110625 | tf_op jit(solution)/shard_map/jit(_where)/select_n | solution.py:130
  202.4 5.1 %multiply_select_fusion.2 = f32[1,4,2,384]{3,1,2,0:T(4,128)S(1)} fusion(f32[4,3,2,32,384]{4,0,2,3,1:T(4,128)S(1)} %fusion.8, f32[]{:T(128)} %bitcast.52, f32[]{:T(128)} %bitcast.51, f32[]{:T(128)} %bitcast.50, f32[]{:T(128)} %bitcast.49, f32[]{:T(128)} %bitcast.48, f32[]{:T(128)} %bitcast.47, f32[]{:T(128)} %bitcast.46, f32[]{:T(128)} %bitcast.45, pred[]{:T(512)S(6)} %eq.25), kind=kLoop, calls=%fused_computation.127 | loop fusion | flops 52224 | bytes 110625 | tf_op jit(solution)/shard_map/jit(_where)/select_n | solution.py:129
  207.7 76.1 %psum.7 = f32[2,4,2,64]{3,1,2,0:T(4,128)S(1)} all-reduce(f32[2,4,2,64]{3,1,2,0:T(4,128)S(1)} %fusion.35), channel_id=1, replica_groups=mesh['wall'=16,'span'=16] {'wall','span'}, use_global_device_ids=true, to_apply=%region_0.1 | all-reduce | flops 1024 | bytes 8192 | tf_op jit(solution)/shard_map/psum | solution.py:134
  (86 shorter events, 25.0 us)
Async XLA Ops:
  3.8 11.7 %copy-start = (f32[4,3,2,32,384]{4,3,2,1,0:T(8,128)S(1)}, f32[4,3,2,32,384]{4,3,2,1,0:T(8,128)}, u32[]{:S(2)}) copy-start(f32[4,3,2,32,384]{4,3,2,1,0:T(8,128)} %param.8) | copy-start | bytes 3538948
  3.8 41.2 %all-to-all-start = ((f32[12,2,32,384]{3,1,0,2:T(2,128)}), f32[12,2,32,384]{3,1,0,2:T(2,128)S(1)}, u32[]{:S(2)}, u32[]{:S(2)}) async-start(f32[12,2,32,384]{3,1,0,2:T(2,128)} %bitcast.18), calls=%async_computation | async-start | bytes 2359296 | tf_op jit(solution)/shard_map/all_to_all | solution.py:106
  17.2 101.0 %collective-permute-start = (f32[4,3,2,7,384]{4,0,2,3,1:T(4,128)}, f32[4,3,2,7,384]{4,0,2,3,1:T(4,128)}, u32[]{:S(2)}, u32[]{:S(2)}) collective-permute-start(f32[4,3,2,7,384]{4,0,2,3,1:T(4,128)} %get-tuple-element.32), channel_id=1, source_target_pairs={{0,16},{16,32},{32,48},{48,64},{64,80},{80,96},{96,112},{112,128},... | collective-permute-start | bytes 774152 | tf_op jit(solution)/shard_map/ppermute | solution.py:22
  20.3 101.0 %collective-permute-start.1 = (f32[4,3,2,7,384]{4,0,2,3,1:T(4,128)}, f32[4,3,2,7,384]{4,0,2,3,1:T(4,128)}, u32[]{:S(2)}, u32[]{:S(2)}) collective-permute-start(f32[4,3,2,7,384]{4,0,2,3,1:T(4,128)} %get-tuple-element.33), channel_id=1, source_target_pairs={{16,0},{32,16},{48,32},{64,48},{80,64},{96,80},{112,96},{128,112},... | collective-permute-start | bytes 774152 | tf_op jit(solution)/shard_map/ppermute | solution.py:25
  107.7 6.7 %copy-start.23 = (s32[4]{0:T(128)S(1)}, s32[4]{0:T(128)}, u32[]{:S(2)}) copy-start(s32[4]{0:T(128)} %param.12) | copy-start | bytes 52
  107.7 6.7 %copy-start.21 = (f32[2,32]{1,0:T(2,128)S(1)}, f32[2,32]{1,0:T(2,128)}, u32[]{:S(2)}) copy-start(f32[2,32]{1,0:T(2,128)} %param.9) | copy-start | bytes 772
  107.7 36.3 %all-to-all-start.1 = ((f32[16,1,18432]{2,1,0:T(1,128)}), f32[16,1,18432]{2,1,0:T(1,128)}, u32[]{:S(2)}, u32[]{:S(2)}) async-start(f32[16,1,18432]{2,1,0:T(1,128)} %reshape.465), calls=%async_computation.1 | async-start | bytes 2359296 | tf_op jit(solution)/shard_map/all_to_all | solution.py:108
  115.2 1.3 copy-start.8
  117.3 3.0 %copy-start.1 = (f32[4,3,2,32,384]{4,3,2,1,0:T(8,128)S(1)}, f32[4,3,2,32,384]{4,3,2,1,0:T(8,128)}, u32[]{:S(2)}) copy-start(f32[4,3,2,32,384]{4,3,2,1,0:T(8,128)} %param.8) | copy-start | bytes 3538948
  118.2 1.0 copy-start.3
  188.8 2.4 copy-start.2
  188.8 2.4 copy-start.4
  188.8 2.5 copy-start.10
  188.8 2.5 copy-start.11
  188.9 2.5 copy-start.12
  188.9 2.5 copy-start.13
  188.9 2.5 copy-start.14
  188.9 2.5 copy-start.15
  188.9 2.5 copy-start.16
  188.9 2.5 copy-start.17
  188.9 2.5 copy-start.18
  188.9 2.5 copy-start.19
  188.9 2.5 copy-start.20
  195.9 11.6 %copy-start.22 = (s32[384]{0:T(512)S(1)}, s32[384]{0:T(512)}, u32[]{:S(2)}) copy-start(s32[384]{0:T(512)} %param.13) | copy-start | bytes 4612
  (4 other events, 3.2 us)
where the time goes:
time: 286 us; the launch traced here: 284 us
  local copies, waits for them, and re-layouts  90.8 us (32%)
  blocking collectives  76.1 us (27%)
  waiting for transfers between devices  43.1 us (15%)
  other arithmetic  35.3 us (12%)
  starting transfers between devices  23.4 us (8%)
  matrix products  14.5 us (5%)
    psum x1, blocking collectives, on_device(): wall_grad = lax.psum(partial_grad, ('wall', 'span'))  76.1 us
    unnamed x55, local copies, waits for them, and re-layouts  58.4 us
    all_to_all x1, waiting for transfers between devices, on_device(): lax.all_to_all(spectral_lines, 'span', split_axis=3, concat_axis=2, tiled...  21.7 us
    all_to_all x1, waiting for transfers between devices, on_device(): lax.all_to_all(flattened, 'span', split_axis=2, concat_axis=3, tiled=True)  21.4 us
    all_to_all x3, local copies, waits for them, and re-layouts, on_device(): lax.all_to_all(spectral_lines, 'span', split_axis=3, concat_axis=2, tiled...  14 us
    unnamed x1, other arithmetic  11.8 us
    all_to_all x1, starting transfers between devices, on_device(): lax.all_to_all(flattened, 'span', split_axis=2, concat_axis=3, tiled=True)  11.7 us
    another operation x2, local copies, waits for them, and re-layouts, spanwise_operator(): return jnp.stack([result_real, result_imag], axis=1)  9.1 us
  transfers between devices with their start and end apart: 4, of which 2 were waited for; matrix products, arithmetic and copies ran while one was open for 25% of the time, Pallas kernels for 0%

commit v1 on v0

v1 whole, which is shorter than its diff:
```python
import math

import jax
import jax.numpy as jnp
import numpy as np
from jax import lax
from jax.experimental import pallas as pl
from jax.experimental.pallas import tpu as pltpu
from jax.sharding import PartitionSpec as P

MESH = pl.DeviceIdType.MESH
MODES, COMPS, ROWS, COLS = 4, 3, 32, 384
WALLS, SPANS = 16, 16
STEN = 15
PATCH = 64
NZ = SPANS * COLS
INNER = 128
OUTER = NZ // INNER
CUTOFF = NZ // 3
VIS = 0.5
TAU = 0.25

OFFSETS = sorted(
    [(hi, z) for hi in range(2) for z in range(8) if hi or z],
    key=lambda o: (2 * o[0] + min(o[1], 8 - o[1]), o),
)


def tables():
    outer = np.array([next(k for k in range(OUTER) if k % 16 == i // 3 and k % 3 == i % 3) for i in range(OUTER)])
    inner = np.arange(INNER)
    angle = 2.0 * np.pi * (outer[:, None] * inner[None, :] % NZ) / NZ
    twist = np.stack([np.cos(angle), np.sin(angle)], axis=1)
    wave = outer[:, None] + OUTER * inner[None, :]
    signed = np.where(wave > NZ // 2, wave - NZ, wave)
    factor = np.where(np.abs(signed) < CUTOFF, -VIS * (signed / CUTOFF) ** 2, 0.0) / NZ
    angle = 2.0 * np.pi * (inner[:, None] * inner[None, :] % INNER) / INNER
    c, s = np.cos(angle), np.sin(angle)
    pair = []
    for table in (np.block([[c, -s], [s, c]]), np.block([[c, s], [-s, c]])):
        high = table.astype(np.float32).astype(jnp.bfloat16)
        low = (table - high.astype(np.float64)).astype(np.float32).astype(jnp.bfloat16)
        pair.append(np.stack([high, low]))
    rows = np.concatenate([twist, factor[:, None]], axis=1).astype(np.float32)
    return np.stack(pair), rows


def times(value, cos, sin):
    re, im = value
    half = math.sqrt(0.5)
    if abs(sin) < 1e-12:
        return (re, im) if cos > 0 else (-re, -im)
    if abs(cos) < 1e-12:
        return (im, -re) if sin > 0 else (-im, re)
    if abs(abs(cos) - half) < 1e-12 and abs(abs(sin) - half) < 1e-12:
        a, b = math.copysign(half, cos), math.copysign(half, sin)
        if a == b:
            return ((re + im) * a, (im - re) * a)
        return ((re - im) * a, (im + re) * a)
    return (re * cos + im * sin, im * cos - re * sin)


def transform(values):
    n = len(values)
    if n == 1:
        return values
    even, odd = transform(values[0::2]), transform(values[1::2])
    first, second = [], []
    for k in range(n // 2):
        a = 2.0 * math.pi * k / n
        t = times(odd[k], math.cos(a), math.sin(a))
        first.append((even[k][0] + t[0], even[k][1] + t[1]))
        second.append((even[k][0] - t[0], even[k][1] - t[1]))
    return first + second


def transform_three(x):
    (ar, ai), (br, bi), (cr, ci) = x
    sr, si, dr, di = br + cr, bi + ci, br - cr, bi - ci
    mr, mi = ar - 0.5 * sr, ai - 0.5 * si
    h = math.sqrt(0.75)
    return [(ar + sr, ai + si), (mr + h * di, mi - h * dr), (mr - h * di, mi + h * dr)]


def swap(values):
    return [(im, re) for re, im in values]


def multiply(values, pair_ref, which):
    high = values.astype(jnp.bfloat16)
    low = (values - high.astype(jnp.float32)).astype(jnp.bfloat16)
    out = jnp.dot(high, pair_ref[which, 0], preferred_element_type=jnp.float32)
    out += jnp.dot(low, pair_ref[which, 0], preferred_element_type=jnp.float32)
    out += jnp.dot(high, pair_ref[which, 1], preferred_element_type=jnp.float32)
    return out


def filter_lines(c, recv, ret, work, mid, pair, trig):
    def lanes(j):
        return slice(INNER * j, INNER * (j + 1))

    for j in range(3):
        order = [(i + 5 * j) % 16 for i in range(16)]
        out = transform([(recv[c, s, 0, :, lanes(j)], recv[c, s, 1, :, lanes(j)]) for s in order])
        for k in range(16):
            work[3 * k + j, :, :INNER], work[3 * k + j, :, INNER:] = out[k]
    for k in range(16):
        out = transform_three([(work[3 * k + j, :, :INNER], work[3 * k + j, :, INNER:]) for j in range(3)])
        for i, (re, im) in enumerate(out):
            cos, sin = trig[3 * k + i, 0:1, :], trig[3 * k + i, 1:2, :]
            mid[3 * k + i, :, :INNER] = re * cos + im * sin
            mid[3 * k + i, :, INNER:] = im * cos - re * sin
    modes = multiply(mid[...].reshape(OUTER * 8, 2 * INNER), pair, 0).reshape(OUTER, 8, 2 * INNER)
    work[...] = modes
    for k in range(OUTER):
        factor = trig[k, 2:3, :]
        mid[k, :, :INNER] = work[k, :, :INNER] * factor
        mid[k, :, INNER:] = work[k, :, INNER:] * factor
    work[...] = multiply(mid[...].reshape(OUTER * 8, 2 * INNER), pair, 1).reshape(OUTER, 8, 2 * INNER)
    for k in range(16):
        values = []
        for i in range(3):
            re, im = work[3 * k + i, :, :INNER], work[3 * k + i, :, INNER:]
            cos, sin = trig[3 * k + i, 0:1, :], trig[3 * k + i, 1:2, :]
            values.append((re * cos - im * sin, im * cos + re * sin))
        out = swap(transform_three(swap(values)))
        for j in range(3):
            mid[3 * k + j, :, :INNER], mid[3 * k + j, :, INNER:] = out[j]
    for j in range(3):
        order = [(i + 5 * j) % 16 for i in range(16)]
        out = swap(transform(swap([(mid[3 * k + j, :, :INNER], mid[3 * k + j, :, INNER:]) for k in range(16)])))
        for i, s in enumerate(order):
            ret[c, s, 0, :, lanes(j)], ret[c, s, 1, :, lanes(j)] = out[i]


def local_terms(c, padded, base, coef, wave_ref):
    def body(i, carry):
        m, j = i // 3, i % 3
        lanes = pl.ds(pl.multiple_of(j * INNER, INNER), INNER)
        rate = TAU * 0.25 * wave_ref[m].astype(jnp.float32)
        for octet in range(ROWS // 8):
            rows = slice(8 * octet, 8 * octet + 8)
            sums = []
            for p in range(2):
                total = jnp.zeros((8, INNER), jnp.float32)
                for s in range(STEN):
                    total += coef[s, rows, :] * padded[m, c, p, 8 * octet + 1 + s : 8 * octet + 9 + s, lanes]
                sums.append(total)
            here = slice(8 * octet + 8, 8 * octet + 16)
            re, im = padded[m, c, 0, here, lanes], padded[m, c, 1, here, lanes]
            turn = rate * coef[STEN, rows, :]
            sums[0] += re - turn * im
            sums[1] += im + turn * re
            if c == 1:
                couple = TAU * coef[STEN + 1, rows, :]
                for p in range(2):
                    sums[p] -= couple * padded[m, 0, p, here, lanes]
            for p in range(2):
                base[m, c, p, rows, lanes] = sums[p]
        return carry

    lax.fori_loop(0, MODES * 3, body, 0)


def kernel(
    field, mean_flow, d2_coef, wall_coef, kx_index, patch_of, pair_hbm, trig_hbm,
    base_out, spw, grad_out,
    padded, base, recv, ret, work, mid, pair, trig, coef, turned, flow, sten, wc, kx, patch, edge, grads, shares,
    load_sem, own_sem, back_sem, f_send, f_recv, r_send, r_recv, h_send, h_recv, s_send, s_recv, g_send, g_recv,
    out_sem, edge_sem,
):
    w, me = lax.axis_index("wall"), lax.axis_index("span")
    at_low, at_high = w == 0, w == WALLS - 1
    at_edge = jnp.logical_or(at_low, at_high)

    def span_of(offset, sign=1):
        hi = lax.rem(me // 8 + offset[0], 2)
        return hi * 8 + lax.rem(lax.rem(me, 8) + 8 + sign * offset[1], 8)

    loads = [
        pltpu.make_async_copy(field, padded.at[:, :, :, pl.ds(8, ROWS), :], load_sem.at[0]),
        pltpu.make_async_copy(mean_flow, flow, load_sem.at[1]),
        pltpu.make_async_copy(d2_coef, sten, load_sem.at[2]),
        pltpu.make_async_copy(wall_coef, wc, load_sem.at[3]),
        pltpu.make_async_copy(kx_index, kx, load_sem.at[4]),
        pltpu.make_async_copy(patch_of, patch, load_sem.at[5]),
        pltpu.make_async_copy(pair_hbm, pair, load_sem.at[6]),
        pltpu.make_async_copy(trig_hbm, trig, load_sem.at[7]),
    ]

    barrier = pltpu.get_barrier_semaphore()
    for offset in OFFSETS:
        pl.semaphore_signal(barrier, inc=1, device_id=(w, span_of(offset)), device_id_type=MESH)

    def greet(wall):
        pl.semaphore_signal(barrier, inc=1, device_id=(wall, me), device_id_type=MESH)

    pl.when(w > 0)(lambda: greet(w - 1))
    pl.when(w < WALLS - 1)(lambda: greet(w + 1))
    pl.when(w > 1)(lambda: greet(0))
    pl.when(w < WALLS - 2)(lambda: greet(WALLS - 1))
    for load in loads:
        load.start()
    pl.when(at_edge)(lambda: pl.semaphore_wait(barrier, SPANS - 1 + WALLS - 1))
    pl.when(jnp.logical_not(at_edge))(lambda: pl.semaphore_wait(barrier, SPANS - 1 + 2))

    def block(t, c):
        return (t // 4, c, slice(None), pl.ds(pl.multiple_of(8 * lax.rem(t, 4), 8), 8), slice(None))

    def forward(c, t, slot):
        return pltpu.make_async_remote_copy(
            src_ref=field.at[block(t, c)], dst_ref=recv.at[c, slot], send_sem=f_send.at[c, t],
            recv_sem=f_recv.at[c, slot], device_id=(w, t), device_id_type=MESH)

    def backward(c, t, slot):
        return pltpu.make_async_remote_copy(
            src_ref=ret.at[c, t], dst_ref=spw.at[block(slot, c)], send_sem=r_send.at[c, t],
            recv_sem=r_recv.at[c, slot], device_id=(w, t), device_id_type=MESH)

    def own(c):
        return pltpu.make_async_copy(field.at[block(me, c)], recv.at[c, me], own_sem.at[c])

    def own_back(c):
        return pltpu.make_async_copy(ret.at[c, me], spw.at[block(me, c)], back_sem.at[c])

    def send_lines(c):
        for offset in OFFSETS:
            forward(c, span_of(offset), me).start()
        own(c).start()

    def take_lines(c):
        for offset in OFFSETS:
            forward(c, me, span_of(offset, -1)).wait_recv()
        own(c).wait()

    def send_back(c):
        for offset in OFFSETS:
            backward(c, span_of(offset), me).start()
        own_back(c).start()

    def take_back(c):
        for offset in OFFSETS:
            backward(c, me, span_of(offset, -1)).wait_recv()
        own_back(c).wait()

    def halo(up):
        src = pl.ds(ROWS - 8 if up else 0, 8)
        dst = pl.ds(0 if up else ROWS + 8, 8)
        return pltpu.make_async_remote_copy(
            src_ref=field.at[:, :, :, src, :], dst_ref=padded.at[:, :, :, dst, :], send_sem=h_send.at[int(up)],
            recv_sem=h_recv.at[int(up)], device_id=(w + 1 if up else w - 1, me), device_id_type=MESH)

    send_lines(0)
    pl.when(w < WALLS - 1)(lambda: halo(True).start())
    pl.when(w > 0)(lambda: halo(False).start())
    send_lines(1)

    @pl.when(at_low)
    def _():
        padded[:, :, :, 0:8, :] = jnp.zeros((MODES, COMPS, 2, 8, COLS), jnp.float32)

    @pl.when(at_high)
    def _():
        padded[:, :, :, ROWS + 8 :, :] = jnp.zeros((MODES, COMPS, 2, 8, COLS), jnp.float32)

    for load in loads:
        load.wait()
    turned[...] = jnp.zeros((INNER, INNER), jnp.float32)
    turned[0:STEN, 0:ROWS] = sten[...]
    turned[STEN : STEN + 2, 0:ROWS] = flow[...]
    columns = turned[...].T
    for k in range(STEN + 2):
        coef[k] = jnp.broadcast_to(columns[0:ROWS, k : k + 1], (ROWS, INNER))

    pl.when(w > 0)(lambda: halo(True).wait_recv())
    pl.when(w < WALLS - 1)(lambda: halo(False).wait_recv())
    local_terms(0, padded, base, coef, kx)

    take_lines(0)
    filter_lines(0, recv, ret, work, mid, pair, trig)
    send_back(0)
    send_lines(2)

    local_terms(1, padded, base, coef, kx)
    take_lines(1)
    filter_lines(1, recv, ret, work, mid, pair, trig)

    def share(t, slot):
        return pltpu.make_async_remote_copy(
            src_ref=grads.at[2], dst_ref=shares.at[slot], send_sem=s_send.at[t], recv_sem=s_recv.at[slot],
            device_id=(w, t), device_id_type=MESH)

    take_back(0)

    @pl.when(at_edge)
    def _():
        rows = pl.ds(pl.multiple_of(jnp.where(at_low, 0, ROWS - 8), 8), 8)
        copy = pltpu.make_async_copy(spw.at[:, 0, :, rows, :], edge, edge_sem)
        copy.start()
        copy.wait()
        line = lax.broadcasted_iota(jnp.int32, (8, COLS), 0)
        weight = jnp.zeros((8, COLS), jnp.float32)
        for j in range(8):
            weight = jnp.where(line == j, jnp.where(at_low, wc[0, j], wc[1, 7 - j]), weight)
        patches = (lax.broadcasted_iota(jnp.int32, (INNER, COLS), 0) == patch[...]).astype(jnp.bfloat16)
        sums = []
        for m in range(MODES):
            for p in range(2):
                values = weight * (base[m, 0, p, rows, :] + edge[m, p])
                sums.append(jnp.sum(values, axis=0, keepdims=True))
        rest = jnp.concatenate(sums, axis=0)
        total = jnp.zeros((8, INNER), jnp.float32)
        for _ in range(3):
            part = rest.astype(jnp.bfloat16)
            rest = rest - part.astype(jnp.float32)
            total += lax.dot_general(part, patches, (((1,), (1,)), ((), ())), preferred_element_type=jnp.float32)
        grads[2] = total
        for offset in OFFSETS:
            share(span_of(offset), me).start()

    send_back(1)
    local_terms(2, padded, base, coef, kx)
    base_copy = pltpu.make_async_copy(base, base_out, out_sem.at[0])
    base_copy.start()
    take_lines(2)
    filter_lines(2, recv, ret, work, mid, pair, trig)

    def spread(side, t):
        return pltpu.make_async_remote_copy(
            src_ref=grads.at[side], dst_ref=grads.at[side], send_sem=g_send.at[t], recv_sem=g_recv.at[side],
            device_id=(t, me), device_id_type=MESH)

    @pl.when(at_edge)
    def _():
        for offset in OFFSETS:
            share(me, span_of(offset, -1)).wait_recv()
        shares[me] = grads[2]
        total = shares[0]
        for s in range(1, SPANS):
            total += shares[s]
        grads[jnp.where(at_low, 0, 1)] = total

    @pl.when(at_low)
    def _():
        for t in range(1, WALLS):
            spread(0, t).start()

    @pl.when(at_high)
    def _():
        for t in range(WALLS - 1):
            spread(1, t).start()

    send_back(2)
    take_back(1)
    pl.when(jnp.logical_not(at_low))(lambda: spread(0, w).wait_recv())
    pl.when(jnp.logical_not(at_high))(lambda: spread(1, w).wait_recv())
    grad_copy = pltpu.make_async_copy(grads.at[pl.ds(0, 2)], grad_out, out_sem.at[1])
    grad_copy.start()
    take_back(2)
    for c in range(COMPS):
        for offset in OFFSETS:
            forward(c, span_of(offset), me).wait_send()
            backward(c, span_of(offset), me).wait_send()
    pl.when(w < WALLS - 1)(lambda: halo(True).wait_send())
    pl.when(w > 0)(lambda: halo(False).wait_send())

    @pl.when(at_edge)
    def _():
        for offset in OFFSETS:
            share(span_of(offset), me).wait_send()

    @pl.when(at_low)
    def _():
        for t in range(1, WALLS):
            spread(0, t).wait_send()

    @pl.when(at_high)
    def _():
        for t in range(WALLS - 1):
            spread(1, t).wait_send()

    base_copy.wait()
    grad_copy.wait()


def on_device(field, mean_flow, d2_coef, wall_coef, kx_index, patch_of):
    pair, trig = tables()
    whole = (MODES, COMPS, 2, ROWS, COLS)
    dma = pltpu.SemaphoreType.DMA
    hbm = pl.BlockSpec(memory_space=pl.ANY)
    base, spanwise, grads = pl.pallas_call(
        kernel,
        out_shape=[
            jax.ShapeDtypeStruct(whole, jnp.float32),
            jax.ShapeDtypeStruct(whole, jnp.float32),
            jax.ShapeDtypeStruct((2, 8, INNER), jnp.float32),
        ],
        in_specs=[hbm] * 8,
        out_specs=[hbm] * 3,
        scratch_shapes=[
            pltpu.VMEM((MODES, COMPS, 2, ROWS + 16, COLS), jnp.float32),
            pltpu.VMEM(whole, jnp.float32),
            pltpu.VMEM((COMPS, SPANS, 2, 8, COLS), jnp.float32),
            pltpu.VMEM((COMPS, SPANS, 2, 8, COLS), jnp.float32),
            pltpu.VMEM((OUTER, 8, 2 * INNER), jnp.float32),
            pltpu.VMEM((OUTER, 8, 2 * INNER), jnp.float32),
            pltpu.VMEM((2, 2, 2 * INNER, 2 * INNER), jnp.bfloat16),
            pltpu.VMEM((OUTER, 3, INNER), jnp.float32),
            pltpu.VMEM((STEN + 2, ROWS, INNER), jnp.float32),
            pltpu.VMEM((INNER, INNER), jnp.float32),
            pltpu.VMEM((2, ROWS), jnp.float32),
            pltpu.VMEM((STEN, ROWS), jnp.float32),
            pltpu.SMEM((2, 8), jnp.float32),
            pltpu.SMEM((MODES,), jnp.int32),
            pltpu.VMEM((1, COLS), jnp.int32),
            pltpu.VMEM((MODES, 2, 8, COLS), jnp.float32),
            pltpu.VMEM((3, 8, INNER), jnp.float32),
            pltpu.VMEM((SPANS, 8, INNER), jnp.float32),
            dma((8,)),
            dma((COMPS,)),
            dma((COMPS,)),
            dma((COMPS, SPANS)),
            dma((COMPS, SPANS)),
            dma((COMPS, SPANS)),
            dma((COMPS, SPANS)),
            dma((2,)),
            dma((2,)),
            dma((SPANS,)),
            dma((SPANS,)),
            dma((WALLS,)),
            dma((2,)),
            dma((2,)),
            dma,
        ],
        compiler_params=pltpu.CompilerParams(collective_id=0, has_side_effects=True),
    )(field, mean_flow, d2_coef, wall_coef, kx_index, patch_of.reshape(1, COLS), pair, trig)
    new_field = base + spanwise
    wall_grad = grads[:, :, :PATCH].reshape(2, MODES, 2, PATCH)
    return new_field, wall_grad


def solution(mesh):
    return jax.shard_map(
        on_device,
        mesh=mesh,
        in_specs=(
            P(None, None, None, "wall", "span"),
            P(None, "wall"),
            P(None, "wall"),
            P(),
            P(),
            P("span"),
        ),
        out_specs=(P(None, None, None, "wall", "span"), P()),
        check_vma=False,
    )
```

time: 286 us -> 71.1 us (0.25)
  local copies, waits for them, and re-layouts: 90.8 us -> 1.85 us
  blocking collectives: 76.1 us -> 0 us
  Pallas kernels: 0 us -> 65.2 us
  waiting for transfers between devices: 43.1 us -> 0 us
  other arithmetic: 35.3 us -> 2.8 us
  starting transfers between devices: 23.4 us -> 0 us
  matrix products: 14.5 us -> 0 us
    psum x1 -> x0, blocking collectives: 76.1 us -> none  [on_device(): wall_grad = lax.psum(partial_grad, ('wall', 'span'))]
    pallas_call x0 -> x1, Pallas kernels: none -> 65.2 us  [on_device(): pl.pallas_call(kernel, out_shape=[jax.ShapeDtypeStruct(whole, jnp.float32...]
    unnamed x55 -> x3, local copies, waits for them, and re-layouts: 58.4 us -> 0.6 us
    all_to_all x2 -> x0, waiting for transfers between devices: 43.1 us -> none  [the longest x1 21.7 us: on_device(): lax.all_to_all(spectral_lines, 'span', split_axis=3, concat_axis=2, tiled...]
    all_to_all x2 -> x0, starting transfers between devices: 18.3 us -> none  [the longest x1 11.7 us: on_device(): lax.all_to_all(flattened, 'span', split_axis=2, concat_axis=3, tiled=True)]
    all_to_all x5 -> x0, local copies, waits for them, and re-layouts: 17.5 us -> none  [the longest x3 14 us: on_device(): lax.all_to_all(spectral_lines, 'span', split_axis=3, concat_axis=2, tiled...]
    dot_general x17 -> x0, matrix products: 14.5 us -> none  [the longest x4 4.27 us: first_back(): return jnp.einsum('kn,irkm->irnm', table, values, precision=highest)]
    unnamed x1 -> x0, other arithmetic: 11.8 us -> none
  transfers between devices with their start and end apart: 4 -> 0, of which waited for: 2 -> 0; matrix products, arithmetic and copies ran while one was open for 25% -> 0% of each run, Pallas kernels for 0% -> 0%
where the time goes in v1:
time: 71.1 us; the launch traced here: 70.5 us
  Pallas kernels  65.2 us (92%)
  other arithmetic  2.8 us (4%)
  local copies, waits for them, and re-layouts  1.85 us (3%)
    pallas_call x1, Pallas kernels, on_device(): pl.pallas_call(kernel, out_shape=[jax.ShapeDtypeStruct(whole, jnp.float32...  65.2 us
    add x1, other arithmetic, on_device(): new_field = base + spanwise  2.8 us

profile of v1, /device:TPU:1, one launch (start us, length us, event | category | flops | bytes accessed | tf_op | source)
XLA Modules:
  0.0 70.5 jit_solution(2433899147937951344)
XLA Ops:
  0.6 1.2 %reshape.10.patch_of = s32[1,384]{1,0:T(1,128)} reshape(s32[384]{0:T(512)} %param.13) | data formatting | bytes 3072 | tf_op jit(solution)/shard_map/reshape | solution.py:436
  1.9 65.2 %shard_map.95 = (f32[4,3,2,32,384]{4,3,2,1,0:T(8,128)}, f32[4,3,2,32,384]{4,3,2,1,0:T(8,128)}, f32[2,8,128]{2,1,0:T(8,128)}) custom-call(f32[4,3,2,32,384]{4,3,2,1,0:T(8,128)} %field.1, f32[2,32]{1,0:T(2,128)} %mean_flow.1, f32[15,32]{1,0:T(8,128)} %d2_coef.1, f32[2,8]{1,0:T(2,128)} %wall_coef.1, s32[4]{0:T(128)} %kx_index.1, s32[1,384]{1,0:T(1,128)} %reshape.10.patch_of, ...), custom_call_target="tpu_custom_call" | custom-call | tf_op jit(solution)/shard_map/pallas_call | solution.py:391
  67.1 0.0 copy-start
  67.1 2.8 %add.3 = f32[4,3,2,32,384]{4,3,2,1,0:T(8,128)} add(f32[4,3,2,32,384]{4,3,2,1,0:T(8,128)} %get-tuple-element.5, f32[4,3,2,32,384]{4,3,2,1,0:T(8,128)} %get-tuple-element.6) | non-fusion elementwise | flops 294912 | bytes 3538944 | tf_op jit(solution)/shard_map/add | solution.py:437
  69.9 0.0 copy-done
  69.9 0.6 copy.11
Async XLA Ops:
  67.1 2.8 %copy-start = (f32[2,8,128]{2,1,0:T(8,128)S(1)}, f32[2,8,128]{2,1,0:T(8,128)}, u32[]{:S(2)}) copy-start(f32[2,8,128]{2,1,0:T(8,128)} %get-tuple-element.7) | copy-start | bytes 24580

commit v2 on v1

--- a/solution.py
+++ b/solution.py
@@ -183,7 +183,7 @@
         pltpu.make_async_copy(d2_coef, sten, load_sem.at[2]),
         pltpu.make_async_copy(wall_coef, wc, load_sem.at[3]),
         pltpu.make_async_copy(kx_index, kx, load_sem.at[4]),
-        pltpu.make_async_copy(patch_of, patch, load_sem.at[5]),
+        pltpu.make_async_copy(patch_of, patch.at[0], load_sem.at[5]),
         pltpu.make_async_copy(pair_hbm, pair, load_sem.at[6]),
         pltpu.make_async_copy(trig_hbm, trig, load_sem.at[7]),
     ]
@@ -385,9 +385,9 @@
 
 def on_device(field, mean_flow, d2_coef, wall_coef, kx_index, patch_of):
     pair, trig = tables()
+    arrays = (field, mean_flow, d2_coef, wall_coef, kx_index, patch_of, pair, trig)
     whole = (MODES, COMPS, 2, ROWS, COLS)
     dma = pltpu.SemaphoreType.DMA
-    hbm = pl.BlockSpec(memory_space=pl.ANY)
     base, spanwise, grads = pl.pallas_call(
         kernel,
         out_shape=[
@@ -395,8 +395,8 @@
             jax.ShapeDtypeStruct(whole, jnp.float32),
             jax.ShapeDtypeStruct((2, 8, INNER), jnp.float32),
         ],
-        in_specs=[hbm] * 8,
-        out_specs=[hbm] * 3,
+        in_specs=[pl.BlockSpec(memory_space=pl.ANY)] * 8,
+        out_specs=[pl.BlockSpec(memory_space=pl.ANY)] * 3,
         scratch_shapes=[
             pltpu.VMEM((MODES, COMPS, 2, ROWS + 16, COLS), jnp.float32),
             pltpu.VMEM(whole, jnp.float32),
@@ -432,8 +432,8 @@
             dma((2,)),
             dma,
         ],
-        compiler_params=pltpu.CompilerParams(collective_id=0, has_side_effects=True),
-    )(field, mean_flow, d2_coef, wall_coef, kx_index, patch_of.reshape(1, COLS), pair, trig)
+        compiler_params=pltpu.CompilerParams(collective_id=0, has_side_effects=True, vmem_limit_bytes=16 * 2**20),
+    )(*[pltpu.with_memory_space_constraint(jnp.asarray(array), pltpu.HBM) for array in arrays])
     new_field = base + spanwise
     wall_grad = grads[:, :, :PATCH].reshape(2, MODES, 2, PATCH)
     return new_field, wall_grad

time: 71.1 us -> 68.3 us (0.961)
  other arithmetic: 2.8 us -> 1.18 us
  local copies, waits for them, and re-layouts: 1.85 us -> 0.6 us
    add x1, other arithmetic: 2.8 us -> 1.18 us  [on_device(): new_field = base + spanwise]
    reshape x1 -> x0, local copies, waits for them, and re-layouts: 1.25 us -> none  [on_device(): patch_of.reshape(1, COLS)]
where the time goes in v2:
time: 68.3 us; the launch traced here: 67.6 us
  Pallas kernels  65.1 us (95%)
  other arithmetic  1.18 us (2%)
    pallas_call x1, Pallas kernels, on_device(): pl.pallas_call(kernel, out_shape=[jax.ShapeDtypeStruct(whole, jnp.float32...  65.1 us

profile of v2, /device:TPU:1, one launch (start us, length us, event | category | flops | bytes accessed | tf_op | source)
XLA Modules:
  0.0 67.6 jit_solution(11087939679980737278)
XLA Ops:
  0.6 65.1 %shard_map.95 = (f32[4,3,2,32,384]{4,3,2,1,0:T(8,128)S(1)}, f32[4,3,2,32,384]{4,3,2,1,0:T(8,128)S(1)}, f32[2,8,128]{2,1,0:T(8,128)S(1)}) custom-call(f32[4,3,2,32,384]{4,3,2,1,0:T(8,128)} %field.1, f32[2,32]{1,0:T(2,128)} %mean_flow.1, f32[15,32]{1,0:T(8,128)} %d2_coef.1, f32[2,8]{1,0:T(2,128)} %wall_coef.1, s32[4]{0:T(128)} %kx_index.1, s32[384]{0:T(512)} %patch_of.1, ...), custom_call_target="tpu_custom_call" | custom-call | tf_op jit(solution)/shard_map/pallas_call | solution.py:391
  65.8 1.2 %add.3 = f32[4,3,2,32,384]{4,3,2,1,0:T(8,128)} add(f32[4,3,2,32,384]{4,3,2,1,0:T(8,128)S(1)} %get-tuple-element.5, f32[4,3,2,32,384]{4,3,2,1,0:T(8,128)S(1)} %get-tuple-element.6) | non-fusion elementwise | flops 294912 | bytes 3538944 | tf_op jit(solution)/shard_map/add | solution.py:437
  67.0 0.6 copy.11

commit v3 on v2

--- a/solution.py
+++ b/solution.py
@@ -166,7 +166,7 @@
     field, mean_flow, d2_coef, wall_coef, kx_index, patch_of, pair_hbm, trig_hbm,
     base_out, spw, grad_out,
     padded, base, recv, ret, work, mid, pair, trig, coef, turned, flow, sten, wc, kx, patch, edge, grads, shares,
-    load_sem, own_sem, back_sem, f_send, f_recv, r_send, r_recv, h_send, h_recv, s_send, s_recv, g_send, g_recv,
+    load_sem, f_send, f_recv, r_send, r_recv, h_send, h_recv, s_send, s_recv, g_send, g_recv,
     out_sem, edge_sem,
 ):
     w, me = lax.axis_index("wall"), lax.axis_index("span")
@@ -209,19 +209,22 @@
 
     def forward(c, t, slot):
         return pltpu.make_async_remote_copy(
-            src_ref=field.at[block(t, c)], dst_ref=recv.at[c, slot], send_sem=f_send.at[c, t],
-            recv_sem=f_recv.at[c, slot], device_id=(w, t), device_id_type=MESH)
+            src_ref=field.at[block(t, c)], dst_ref=recv.at[c, slot], send_sem=f_send,
+            recv_sem=f_recv.at[c], device_id=(w, t), device_id_type=MESH)
 
     def backward(c, t, slot):
         return pltpu.make_async_remote_copy(
-            src_ref=ret.at[c, t], dst_ref=spw.at[block(slot, c)], send_sem=r_send.at[c, t],
-            recv_sem=r_recv.at[c, slot], device_id=(w, t), device_id_type=MESH)
+            src_ref=ret.at[c, t], dst_ref=spw.at[block(slot, c)], send_sem=r_send,
+            recv_sem=r_recv.at[c], device_id=(w, t), device_id_type=MESH)
+
+    def wait_bytes(ref, sem):
+        pltpu.make_async_copy(ref, ref, sem).wait()
 
     def own(c):
-        return pltpu.make_async_copy(field.at[block(me, c)], recv.at[c, me], own_sem.at[c])
+        return pltpu.make_async_copy(field.at[block(me, c)], recv.at[c, me], f_recv.at[c])
 
     def own_back(c):
-        return pltpu.make_async_copy(ret.at[c, me], spw.at[block(me, c)], back_sem.at[c])
+        return pltpu.make_async_copy(ret.at[c, me], spw.at[block(me, c)], r_recv.at[c])
 
     def send_lines(c):
         for offset in OFFSETS:
@@ -229,9 +232,7 @@
         own(c).start()
 
     def take_lines(c):
-        for offset in OFFSETS:
-            forward(c, me, span_of(offset, -1)).wait_recv()
-        own(c).wait()
+        wait_bytes(recv.at[c], f_recv.at[c])
 
     def send_back(c):
         for offset in OFFSETS:
@@ -239,9 +240,7 @@
         own_back(c).start()
 
     def take_back(c):
-        for offset in OFFSETS:
-            backward(c, me, span_of(offset, -1)).wait_recv()
-        own_back(c).wait()
+        wait_bytes(spw.at[:, c], r_recv.at[c])
 
     def halo(up):
         src = pl.ds(ROWS - 8 if up else 0, 8)
@@ -287,7 +286,7 @@
 
     def share(t, slot):
         return pltpu.make_async_remote_copy(
-            src_ref=grads.at[2], dst_ref=shares.at[slot], send_sem=s_send.at[t], recv_sem=s_recv.at[slot],
+            src_ref=grads.at[2], dst_ref=shares.at[slot], send_sem=s_send, recv_sem=s_recv,
             device_id=(w, t), device_id_type=MESH)
 
     take_back(0)
@@ -327,13 +326,12 @@
 
     def spread(side, t):
         return pltpu.make_async_remote_copy(
-            src_ref=grads.at[side], dst_ref=grads.at[side], send_sem=g_send.at[t], recv_sem=g_recv.at[side],
+            src_ref=grads.at[side], dst_ref=grads.at[side], send_sem=g_send, recv_sem=g_recv.at[side],
             device_id=(t, me), device_id_type=MESH)
 
     @pl.when(at_edge)
     def _():
-        for offset in OFFSETS:
-            share(me, span_of(offset, -1)).wait_recv()
+        wait_bytes(shares.at[pl.ds(0, SPANS - 1)], s_recv)
         shares[me] = grads[2]
         total = shares[0]
         for s in range(1, SPANS):
@@ -356,31 +354,21 @@
     pl.when(jnp.logical_not(at_high))(lambda: spread(1, w).wait_recv())
     grad_copy = pltpu.make_async_copy(grads.at[pl.ds(0, 2)], grad_out, out_sem.at[1])
     grad_copy.start()
-    take_back(2)
-    for c in range(COMPS):
-        for offset in OFFSETS:
-            forward(c, span_of(offset), me).wait_send()
-            backward(c, span_of(offset), me).wait_send()
+
+    wait_bytes(recv.at[:, pl.ds(0, SPANS - 1)], f_send)
     pl.when(w < WALLS - 1)(lambda: halo(True).wait_send())
     pl.when(w > 0)(lambda: halo(False).wait_send())
 
     @pl.when(at_edge)
     def _():
-        for offset in OFFSETS:
-            share(span_of(offset), me).wait_send()
-
-    @pl.when(at_low)
-    def _():
-        for t in range(1, WALLS):
-            spread(0, t).wait_send()
-
-    @pl.when(at_high)
-    def _():
-        for t in range(WALLS - 1):
-            spread(1, t).wait_send()
+        wait_bytes(shares.at[pl.ds(0, SPANS - 1)], s_send)
+
+        wait_bytes(shares.at[pl.ds(0, WALLS - 1)], g_send)
 
     base_copy.wait()
     grad_copy.wait()
+    wait_bytes(ret.at[:, pl.ds(0, SPANS - 1)], r_send)
+    take_back(2)
 
 
 def on_device(field, mean_flow, d2_coef, wall_coef, kx_index, patch_of):
@@ -417,17 +405,15 @@
             pltpu.VMEM((3, 8, INNER), jnp.float32),
             pltpu.VMEM((SPANS, 8, INNER), jnp.float32),
             dma((8,)),
+            dma,
             dma((COMPS,)),
+            dma,
             dma((COMPS,)),
-            dma((COMPS, SPANS)),
-            dma((COMPS, SPANS)),
-            dma((COMPS, SPANS)),
-            dma((COMPS, SPANS)),
             dma((2,)),
             dma((2,)),
-            dma((SPANS,)),
-            dma((SPANS,)),
-            dma((WALLS,)),
+            dma,
+            dma,
+            dma,
             dma((2,)),
             dma((2,)),
             dma,

time: 68.3 us -> 65.8 us (0.963)
  Pallas kernels: 65.1 us -> 62.7 us
    pallas_call x1, Pallas kernels: 65.1 us -> 62.7 us  [on_device(): pl.pallas_call(kernel, out_shape=[jax.ShapeDtypeStruct(whole, jnp.float32...]
where the time goes in v3:
time: 65.8 us; the launch traced here: 65.1 us
  Pallas kernels  62.7 us (95%)
  other arithmetic  1.18 us (2%)
    pallas_call x1, Pallas kernels, on_device(): pl.pallas_call(kernel, out_shape=[jax.ShapeDtypeStruct(whole, jnp.float32...  62.7 us

profile of v3, /device:TPU:1, one launch (start us, length us, event | category | flops | bytes accessed | tf_op | source)
XLA Modules:
  0.0 65.1 jit_solution(12362712721696614153)
XLA Ops:
  0.6 62.7 %shard_map.95 = (f32[4,3,2,32,384]{4,3,2,1,0:T(8,128)S(1)}, f32[4,3,2,32,384]{4,3,2,1,0:T(8,128)S(1)}, f32[2,8,128]{2,1,0:T(8,128)S(1)}) custom-call(f32[4,3,2,32,384]{4,3,2,1,0:T(8,128)} %field.1, f32[2,32]{1,0:T(2,128)} %mean_flow.1, f32[15,32]{1,0:T(8,128)} %d2_coef.1, f32[2,8]{1,0:T(2,128)} %wall_coef.1, s32[4]{0:T(128)} %kx_index.1, s32[384]{0:T(512)} %patch_of.1, ...), custom_call_target="tpu_custom_call" | custom-call | tf_op jit(solution)/shard_map/pallas_call | solution.py:379
  63.3 1.2 %add.3 = f32[4,3,2,32,384]{4,3,2,1,0:T(8,128)} add(f32[4,3,2,32,384]{4,3,2,1,0:T(8,128)S(1)} %get-tuple-element.5, f32[4,3,2,32,384]{4,3,2,1,0:T(8,128)S(1)} %get-tuple-element.6) | non-fusion elementwise | flops 294912 | bytes 3538944 | tf_op jit(solution)/shard_map/add | solution.py:423
  64.5 0.6 copy.11

commit v4 on v3

--- a/solution.py
+++ b/solution.py
@@ -275,14 +275,20 @@
     pl.when(w < WALLS - 1)(lambda: halo(False).wait_recv())
     local_terms(0, padded, base, coef, kx)
 
+    send_lines(2)
+
     take_lines(0)
     filter_lines(0, recv, ret, work, mid, pair, trig)
     send_back(0)
-    send_lines(2)
-
     local_terms(1, padded, base, coef, kx)
     take_lines(1)
     filter_lines(1, recv, ret, work, mid, pair, trig)
+    send_back(1)
+    local_terms(2, padded, base, coef, kx)
+    base_copy = pltpu.make_async_copy(base, base_out, out_sem.at[0])
+    base_copy.start()
+    take_lines(2)
+    filter_lines(2, recv, ret, work, mid, pair, trig)
 
     def share(t, slot):
         return pltpu.make_async_remote_copy(
@@ -317,12 +323,7 @@
         for offset in OFFSETS:
             share(span_of(offset), me).start()
 
-    send_back(1)
-    local_terms(2, padded, base, coef, kx)
-    base_copy = pltpu.make_async_copy(base, base_out, out_sem.at[0])
-    base_copy.start()
-    take_lines(2)
-    filter_lines(2, recv, ret, work, mid, pair, trig)
+    send_back(2)
 
     def spread(side, t):
         return pltpu.make_async_remote_copy(
@@ -348,7 +349,6 @@
         for t in range(WALLS - 1):
             spread(1, t).start()
 
-    send_back(2)
     take_back(1)
     pl.when(jnp.logical_not(at_low))(lambda: spread(0, w).wait_recv())
     pl.when(jnp.logical_not(at_high))(lambda: spread(1, w).wait_recv())

time: 65.8 us -> 65.6 us (level)
  Pallas kernels: 62.7 us -> 62 us
where the time goes in v4:
time: 65.6 us; the launch traced here: 64.4 us
  Pallas kernels  62 us (95%)
  other arithmetic  1.18 us (2%)
    pallas_call x1, Pallas kernels, on_device(): pl.pallas_call(kernel, out_shape=[jax.ShapeDtypeStruct(whole, jnp.float32...  62 us

profile of v4, /device:TPU:1, one launch (start us, length us, event | category | flops | bytes accessed | tf_op | source)
XLA Modules:
  0.0 64.4 jit_solution(3716797340498080334)
XLA Ops:
  0.6 62.0 %shard_map.95 = (f32[4,3,2,32,384]{4,3,2,1,0:T(8,128)S(1)}, f32[4,3,2,32,384]{4,3,2,1,0:T(8,128)S(1)}, f32[2,8,128]{2,1,0:T(8,128)S(1)}) custom-call(f32[4,3,2,32,384]{4,3,2,1,0:T(8,128)} %field.1, f32[2,32]{1,0:T(2,128)} %mean_flow.1, f32[15,32]{1,0:T(8,128)} %d2_coef.1, f32[2,8]{1,0:T(2,128)} %wall_coef.1, s32[4]{0:T(128)} %kx_index.1, s32[384]{0:T(512)} %patch_of.1, ...), custom_call_target="tpu_custom_call" | custom-call | tf_op jit(solution)/shard_map/pallas_call | solution.py:379
  62.7 1.2 %add.3 = f32[4,3,2,32,384]{4,3,2,1,0:T(8,128)} add(f32[4,3,2,32,384]{4,3,2,1,0:T(8,128)S(1)} %get-tuple-element.5, f32[4,3,2,32,384]{4,3,2,1,0:T(8,128)S(1)} %get-tuple-element.6) | non-fusion elementwise | flops 294912 | bytes 3538944 | tf_op jit(solution)/shard_map/add | solution.py:423
  63.8 0.6 copy.11

commit v5 on v4

--- a/solution.py
+++ b/solution.py
@@ -22,7 +22,7 @@
 
 OFFSETS = sorted(
     [(hi, z) for hi in range(2) for z in range(8) if hi or z],
-    key=lambda o: (2 * o[0] + min(o[1], 8 - o[1]), o),
+    key=lambda o: (-min(o[1], 8 - o[1]), -o[0], o),
 )
 
 

time: 65.6 us -> 65.7 us (level); the launches traced: 64.4 us -> 65.7 us
  Pallas kernels: 62 us -> 63.2 us
    pallas_call x1, Pallas kernels: 62 us -> 63.2 us  [on_device(): pl.pallas_call(kernel, out_shape=[jax.ShapeDtypeStruct(whole, jnp.float32...]
where the time goes in v5:
time: 65.7 us
  Pallas kernels  63.2 us (96%)
  other arithmetic  1.18 us (2%)
    pallas_call x1, Pallas kernels, on_device(): pl.pallas_call(kernel, out_shape=[jax.ShapeDtypeStruct(whole, jnp.float32...  63.2 us

profile of v5, /device:TPU:1, one launch (start us, length us, event | category | flops | bytes accessed | tf_op | source)
XLA Modules:
  0.0 65.7 jit_solution(15576112385050745796)
XLA Ops:
  0.6 63.2 %shard_map.95 = (f32[4,3,2,32,384]{4,3,2,1,0:T(8,128)S(1)}, f32[4,3,2,32,384]{4,3,2,1,0:T(8,128)S(1)}, f32[2,8,128]{2,1,0:T(8,128)S(1)}) custom-call(f32[4,3,2,32,384]{4,3,2,1,0:T(8,128)} %field.1, f32[2,32]{1,0:T(2,128)} %mean_flow.1, f32[15,32]{1,0:T(8,128)} %d2_coef.1, f32[2,8]{1,0:T(2,128)} %wall_coef.1, s32[4]{0:T(128)} %kx_index.1, s32[384]{0:T(512)} %patch_of.1, ...), custom_call_target="tpu_custom_call" | custom-call | tf_op jit(solution)/shard_map/pallas_call | solution.py:379
  63.9 1.2 %add.3 = f32[4,3,2,32,384]{4,3,2,1,0:T(8,128)} add(f32[4,3,2,32,384]{4,3,2,1,0:T(8,128)S(1)} %get-tuple-element.5, f32[4,3,2,32,384]{4,3,2,1,0:T(8,128)S(1)} %get-tuple-element.6) | non-fusion elementwise | flops 294912 | bytes 3538944 | tf_op jit(solution)/shard_map/add | solution.py:423
  65.1 0.6 copy.11

commit v6 on v4

--- a/solution.py
+++ b/solution.py
@@ -167,7 +167,7 @@
     base_out, spw, grad_out,
     padded, base, recv, ret, work, mid, pair, trig, coef, turned, flow, sten, wc, kx, patch, edge, grads, shares,
     load_sem, f_send, f_recv, r_send, r_recv, h_send, h_recv, s_send, s_recv, g_send, g_recv,
-    out_sem, edge_sem,
+    out_sem, edge_sem, ready,
 ):
     w, me = lax.axis_index("wall"), lax.axis_index("span")
     at_low, at_high = w == 0, w == WALLS - 1
@@ -197,12 +197,21 @@
 
     pl.when(w > 0)(lambda: greet(w - 1))
     pl.when(w < WALLS - 1)(lambda: greet(w + 1))
-    pl.when(w > 1)(lambda: greet(0))
-    pl.when(w < WALLS - 2)(lambda: greet(WALLS - 1))
+
+    @pl.when(at_low)
+    def _():
+        for t in range(2, WALLS):
+            greet(t)
+
+    @pl.when(at_high)
+    def _():
+        for t in range(WALLS - 2):
+            greet(t)
+
     for load in loads:
         load.start()
-    pl.when(at_edge)(lambda: pl.semaphore_wait(barrier, SPANS - 1 + WALLS - 1))
-    pl.when(jnp.logical_not(at_edge))(lambda: pl.semaphore_wait(barrier, SPANS - 1 + 2))
+    near = [w > 0, w > 1, w < WALLS - 1, w < WALLS - 2]
+    pl.semaphore_wait(barrier, SPANS - 1 + sum(one.astype(jnp.int32) for one in near))
 
     def block(t, c):
         return (t // 4, c, slice(None), pl.ds(pl.multiple_of(8 * lax.rem(t, 4), 8), 8), slice(None))
@@ -253,6 +262,12 @@
     pl.when(w < WALLS - 1)(lambda: halo(True).start())
     pl.when(w > 0)(lambda: halo(False).start())
     send_lines(1)
+
+    def report(wall):
+        pl.semaphore_signal(ready, inc=1, device_id=(wall, me), device_id_type=MESH)
+
+    pl.when(w > 1)(lambda: report(0))
+    pl.when(w < WALLS - 2)(lambda: report(WALLS - 1))
 
     @pl.when(at_low)
     def _():
@@ -338,6 +353,7 @@
         for s in range(1, SPANS):
             total += shares[s]
         grads[jnp.where(at_low, 0, 1)] = total
+        pl.semaphore_wait(ready, WALLS - 2)
 
     @pl.when(at_low)
     def _():
@@ -417,6 +433,7 @@
             dma((2,)),
             dma((2,)),
             dma,
+            pltpu.SemaphoreType.REGULAR,
         ],
         compiler_params=pltpu.CompilerParams(collective_id=0, has_side_effects=True, vmem_limit_bytes=16 * 2**20),
     )(*[pltpu.with_memory_space_constraint(jnp.asarray(array), pltpu.HBM) for array in arrays])

time: 65.6 us -> 67.7 us (1.032); the launches traced: 64.4 us -> 67.6 us
  Pallas kernels: 62 us -> 65.2 us
    pallas_call x1, Pallas kernels: 62 us -> 65.2 us  [on_device(): pl.pallas_call(kernel, out_shape=[jax.ShapeDtypeStruct(whole, jnp.float32...]
where the time goes in v6:
time: 67.7 us; the launch traced here: 67.6 us
  Pallas kernels  65.2 us (96%)
  other arithmetic  1.18 us (2%)
    pallas_call x1, Pallas kernels, on_device(): pl.pallas_call(kernel, out_shape=[jax.ShapeDtypeStruct(whole, jnp.float32...  65.2 us

profile of v6, /device:TPU:1, one launch (start us, length us, event | category | flops | bytes accessed | tf_op | source)
XLA Modules:
  0.0 67.6 jit_solution(2927723167814354808)
XLA Ops:
  0.6 65.2 %shard_map.95 = (f32[4,3,2,32,384]{4,3,2,1,0:T(8,128)S(1)}, f32[4,3,2,32,384]{4,3,2,1,0:T(8,128)S(1)}, f32[2,8,128]{2,1,0:T(8,128)S(1)}) custom-call(f32[4,3,2,32,384]{4,3,2,1,0:T(8,128)} %field.1, f32[2,32]{1,0:T(2,128)} %mean_flow.1, f32[15,32]{1,0:T(8,128)} %d2_coef.1, f32[2,8]{1,0:T(2,128)} %wall_coef.1, s32[4]{0:T(128)} %kx_index.1, s32[384]{0:T(512)} %patch_of.1, ...), custom_call_target="tpu_custom_call" | custom-call | tf_op jit(solution)/shard_map/pallas_call | solution.py:395
  65.8 1.2 %add.3 = f32[4,3,2,32,384]{4,3,2,1,0:T(8,128)} add(f32[4,3,2,32,384]{4,3,2,1,0:T(8,128)S(1)} %get-tuple-element.5, f32[4,3,2,32,384]{4,3,2,1,0:T(8,128)S(1)} %get-tuple-element.6) | non-fusion elementwise | flops 294912 | bytes 3538944 | tf_op jit(solution)/shard_map/add | solution.py:440
  67.0 0.6 copy.11
